TPU v7x, 32 devices: a whole 2x2x4 slice. The times are simulated.
32 devices in a mesh: groups: 2 (over x), tile: 16 (over z, y, core).
Axes of the slice: x: 2, y: 2, z: 4, core: 2. Of those that a mesh axis runs over, the one named last changes fastest.
Arguments:
- grid_tokens: bfloat16 [16384, 512], P(('groups', 'tile')), parts along dimension 0, may hold values from -220 to 220
- obs_features: bfloat16 [65536, 128], P(('groups', 'tile')), parts along dimension 0, may hold values from -45 to 45
- w_obs: bfloat16 [128, 512], replicated, may hold values from -0.5 to 0.5
- b_obs: float32 [512], replicated, may hold values from -4 to 4
- w_query: bfloat16 [512, 512], replicated, may hold values from -0.25 to 0.25
- w_key: bfloat16 [512, 512], replicated, may hold values from -0.25 to 0.25
- w_value: bfloat16 [512, 512], replicated, may hold values from -0.25 to 0.25
- w_out: bfloat16 [512, 512], replicated, may hold values from -0.25 to 0.25
- block_lists: int32 [128, 32], P('groups'), parts along dimension 0, may hold values from 0 to 511, as said below
- block_counts: int32 [128], P('groups'), parts along dimension 0, may hold values from 24 to 32, as said below
- block_position: int32 [1024], P('groups'), parts along dimension 0, may hold values from 0 to 511, as said below
- proc_order: int32 [128], P('groups'), parts along dimension 0, may hold values from 0 to 63, each once
Outputs:
- arranged: bfloat16 [16384, 512], P(('groups', 'tile')), parts along dimension 0
There are 2 independent parts, one for each index of `groups`. A program takes and returns all parts, laid end to end along the dimension named above; an argument that names none is the same for every part. Nothing has to cross between parts.
Inputs may be any that keep to these rules, and one draw needn't show every extreme that they name: `block_lists`: over the entries below block_counts of the 4 tiles t of one device (t // 4 equal), at most 16 name blocks whose storage position // 32 is any one device; in every draw some device has exactly 16 from some device. `block_counts`: some tile uses all 32 entries. `block_position`: A permutation of the storage positions.
All inputs are finite; a program needn't handle non-finite values.
Results may differ from a plain program's by a relative error of at most 0.012.
The roundings to bfloat16 on the way count: a program that leaves them out, or rounds other values in their place, can miss the bound.
Values may be sent and summed in bfloat16 or wider, within the bound.
A program may use at most 128 MiB of HBM per device.

v0:
```python
import functools

import jax
import jax.numpy as jnp
from jax import lax
from jax.experimental import pallas as pl
from jax.experimental.pallas import tpu as pltpu
from jax.sharding import PartitionSpec as P

HEADS = 8
BLOCK = 64
NSEL = 32
TILE_ROWS = 128
CHUNK = 512
NEG = -1e30


def attend_kernel(
    owned,
    list_ref,
    count_ref,
    position_ref,
    grid_ref,
    blocks_ref,
    mean_ref,
    rstd_ref,
    w_obs_ref,
    b_obs_ref,
    w_query_ref,
    w_key_ref,
    w_value_ref,
    w_out_ref,
    out_ref,
    raw,
    keys,
    values,
    copy_sem,
):
    tile = pl.program_id(0)
    tiles = pl.num_programs(0)
    key_span = NSEL * BLOCK
    width = grid_ref.shape[1]
    pair = 2 * (width // HEADS)
    base = lax.axis_index("tile") * tiles if owned else 0

    def fetch(which):
        slot = lax.rem(which, 2)

        def one(j, carry):
            spot = position_ref[list_ref[base + which, j]]
            pltpu.make_async_copy(
                blocks_ref.at[pl.ds(spot * BLOCK, BLOCK), :],
                raw.at[slot, pl.ds(j * BLOCK, BLOCK), :],
                copy_sem.at[slot],
            ).start()
            return carry

        lax.fori_loop(0, NSEL, one, 0)

    @pl.when(tile == 0)
    def _():
        fetch(tile)

    slot = lax.rem(tile, 2)
    pltpu.make_async_copy(
        blocks_ref.at[pl.ds(0, key_span), :], raw.at[slot], copy_sem.at[slot]
    ).wait()

    @pl.when(tile + 1 < tiles)
    def _():
        fetch(tile + 1)

    for start in range(0, key_span, CHUNK):
        rows = pl.ds(start, CHUNK)
        feats = raw[slot, rows, :].astype(jnp.float32)
        normed = ((feats - mean_ref[...]) * rstd_ref[...]).astype(jnp.bfloat16)
        hidden = jnp.dot(normed, w_obs_ref[...], preferred_element_type=jnp.float32)
        hidden = hidden + b_obs_ref[...]
        embedded = jax.nn.gelu(hidden, approximate=True).astype(jnp.bfloat16)
        keys[rows, :] = jnp.dot(
            embedded, w_key_ref[...], preferred_element_type=jnp.float32
        ).astype(jnp.bfloat16)
        values[rows, :] = jnp.dot(
            embedded, w_value_ref[...], preferred_element_type=jnp.float32
        ).astype(jnp.bfloat16)

    queries = jnp.dot(
        grid_ref[...], w_query_ref[...], preferred_element_type=jnp.float32
    ).astype(jnp.bfloat16)
    queries = queries * jnp.bfloat16(1.0 / (width // HEADS) ** 0.5)
    certain = 3 * key_span // 4
    used = count_ref[base + tile] * BLOCK
    key_index = certain + lax.broadcasted_iota(jnp.int32, (1, key_span - certain), 1)
    bias = jnp.where(key_index < used, 0.0, NEG).astype(jnp.float32)
    lane = lax.broadcasted_iota(jnp.int32, (TILE_ROWS, pair), 1)
    first = lane < pair // 2
    zero = jnp.zeros((), jnp.bfloat16)
    parts = []
    for p in range(HEADS // 2):
        columns = slice(p * pair, (p + 1) * pair)
        q = queries[:, columns]
        both = jnp.concatenate([jnp.where(first, q, zero), jnp.where(first, zero, q)], axis=0)
        scores = lax.dot_general(
            both,
            keys[:, columns],
            (((1,), (1,)), ((), ())),
            preferred_element_type=jnp.float32,
        )
        scores = jnp.concatenate([scores[:, :certain], scores[:, certain:] + bias], axis=1)
        peak = jnp.max(scores, axis=-1, keepdims=True)
        expo = jnp.exp(scores - peak)
        totals = jnp.sum(expo, axis=-1, keepdims=True)
        mixed = jnp.dot(
            expo.astype(jnp.bfloat16), values[:, columns], preferred_element_type=jnp.float32
        )
        mixed = mixed / totals
        parts.append(
            jnp.where(first, mixed[:TILE_ROWS], mixed[TILE_ROWS:]).astype(jnp.bfloat16)
        )
    attended = jnp.concatenate(parts, axis=1)
    encoded = jnp.dot(
        attended, w_out_ref[...], preferred_element_type=jnp.float32
    ).astype(jnp.bfloat16)
    out_ref[...] = encoded.reshape(out_ref.shape)


def attend(
    tile_count,
    owned,
    lists,
    counts,
    position,
    grid_tokens,
    blocks,
    mean,
    rstd,
    w_obs,
    b_obs,
    w_query,
    w_key,
    w_value,
    w_out,
):
    rows, width = grid_tokens.shape
    piece = TILE_ROWS // tile_count
    feat = blocks.shape[1]
    key_span = NSEL * BLOCK

    def whole(shape):
        return pl.BlockSpec(shape, lambda t, *_: (0, 0))

    square = whole((width, width))
    return pl.pallas_call(
        functools.partial(attend_kernel, owned),
        grid_spec=pltpu.PrefetchScalarGridSpec(
            num_scalar_prefetch=3,
            grid=(rows // TILE_ROWS,),
            in_specs=[
                pl.BlockSpec((TILE_ROWS, width), lambda t, *_: (t, 0)),
                pl.BlockSpec(memory_space=pl.ANY),
                whole((1, feat)),
                whole((1, feat)),
                whole((feat, width)),
                whole((1, width)),
                square,
                square,
                square,
                square,
            ],
            out_specs=pl.BlockSpec((tile_count, 1, piece, width), lambda t, *_: (0, t, 0, 0)),
            scratch_shapes=[
                pltpu.VMEM((2, key_span, feat), jnp.bfloat16),
                pltpu.VMEM((key_span, width), jnp.bfloat16),
                pltpu.VMEM((key_span, width), jnp.bfloat16),
                pltpu.SemaphoreType.DMA((2,)),
            ],
        ),
        out_shape=jax.ShapeDtypeStruct(
            (tile_count, rows // TILE_ROWS, piece, width), jnp.bfloat16
        ),
        compiler_params=pltpu.CompilerParams(dimension_semantics=("arbitrary",)),
        cost_estimate=pl.CostEstimate(
            flops=12_000_000_000, bytes_accessed=6_000_000, transcendentals=12_000_000
        ),
    )(
        lists,
        counts,
        position,
        grid_tokens,
        blocks,
        mean,
        rstd,
        w_obs,
        b_obs[None],
        w_query,
        w_key,
        w_value,
        w_out,
    )


MESH = pl.DeviceIdType.MESH


def greet_all(me, count):
    barrier = pltpu.get_barrier_semaphore()

    def one(k, carry):
        peer = lax.rem(me + k, count)
        pl.semaphore_signal(barrier, inc=1, device_id={"tile": peer}, device_id_type=MESH)
        return carry

    lax.fori_loop(1, count, one, 0)
    pl.semaphore_wait(barrier, count - 1)


def gather_kernel(
    lines, obs_ref, all_ref, mean_ref, rstd_ref, part, parts, sends, recvs, part_sends, part_recvs, own_sem
):
    count = 4 * lines
    me = lax.axis_index("tile")
    z, y, c = me // 4, lax.rem(me // 2, 2), lax.rem(me, 2)
    rows = obs_ref.shape[0]
    half = rows // 2
    odd = lax.rem(z, 2)

    def index(zz, yy, cc):
        return (zz * 2 + yy) * 2 + cc

    down, up = index(z - 1, y, c), index(z + 1, y, c)
    across, beside = index(z, 1 - y, c), index(z, y, 1 - c)
    buddy_z = z + 1 - 2 * odd
    buddy = index(buddy_z, y, c)
    targets = (down, up, across, beside, buddy)

    def place(block, h):
        return all_ref.at[pl.ds(pl.multiple_of(block * rows + h * half, half), half), :]

    def send(block, h, way, own=False):
        return pltpu.make_async_remote_copy(
            src_ref=obs_ref.at[pl.ds(h * half, half), :] if own else place(block, h),
            dst_ref=place(block, h),
            send_sem=sends.at[way, 2 * block + h],
            recv_sem=recvs.at[2 * block + h],
            device_id={"tile": targets[way]},
            device_id_type=MESH,
        )

    greet_all(me, count)
    for h in range(2):

        @pl.when(z > 0)
        def _():
            send(me, h, 0, True).start()

        @pl.when(z < lines - 1)
        def _():
            send(me, h, 1, True).start()

        send(me, h, 2, True).start()
        send(me, h, 3, True).start()
    own = pltpu.make_async_copy(
        obs_ref, all_ref.at[pl.ds(pl.multiple_of(me * rows, rows), rows), :], own_sem
    )
    own.start()

    feats = obs_ref[...].astype(jnp.float32)
    part[...] = jnp.zeros_like(part)
    part[0:1, :] = jnp.sum(feats, axis=0, keepdims=True)
    part[1:2, :] = jnp.sum(feats * feats, axis=0, keepdims=True)
    parts[pl.ds(me, 1)] = part[...][None]

    for hop in range(1, lines + 1):
        for h in range(2):
            if hop < lines:
                from_up, from_down = index(z + hop, y, c), index(z - hop, y, c)

                @pl.when(z + hop < lines)
                def _():
                    send(from_up, h, 3).wait_recv()

                    @pl.when(z > 0)
                    def _():
                        send(from_up, h, 0).start()

                    if hop == 1 and h == 1:

                        @pl.when(odd == 1)
                        def _():
                            send(from_up, h, 2).start()

                    else:
                        send(from_up, h, 2).start()
                    send(from_up, h, 3).start()

                @pl.when(z - hop >= 0)
                def _():
                    send(from_down, h, 3).wait_recv()

                    @pl.when(z < lines - 1)
                    def _():
                        send(from_down, h, 1).start()

                    if hop == 1 and h == 1:

                        @pl.when(odd == 0)
                        def _():
                            send(from_down, h, 2).start()

                    else:
                        send(from_down, h, 2).start()
                    send(from_down, h, 3).start()

            far = hop - 1
            for sign in (1, -1) if far else (1,):
                other = index(z + sign * far, 1 - y, c)

                @pl.when((z + sign * far >= 0) & (z + sign * far < lines))
                def _():
                    send(other, h, 3).wait_recv()
                    if far == 0 and h == 1:
                        send(other, h, 4).start()
                    send(other, h, 3).start()

        if hop == 1:

            def share(k, carry):
                peer = lax.rem(me + k, count)
                pltpu.make_async_remote_copy(
                    src_ref=part,
                    dst_ref=parts.at[me],
                    send_sem=part_sends.at[k],
                    recv_sem=part_recvs.at[me],
                    device_id={"tile": peer},
                    device_id_type=MESH,
                ).start()
                return carry

            lax.fori_loop(1, count, share, 0)

    def gathered(k, carry):
        peer = lax.rem(me + k, count)
        copy = pltpu.make_async_remote_copy(
            src_ref=part,
            dst_ref=parts.at[peer],
            send_sem=part_sends.at[k],
            recv_sem=part_recvs.at[peer],
            device_id={"tile": peer},
            device_id_type=MESH,
        )
        copy.wait_send()
        copy.wait_recv()
        return carry

    lax.fori_loop(1, count, gathered, 0)
    sums = jnp.sum(parts[...], axis=0)
    total = rows * count
    mean = sums[0:1, :] / total
    mean_ref[...] = mean
    rstd_ref[...] = lax.rsqrt(sums[1:2, :] / total - mean * mean + 1e-05)

    for zz in range(lines):
        held = index(zz, y, c)
        for h in range(2):
            for yy in range(2):
                send(index(zz, yy, 1 - c), h, 3).wait_recv()
                send(index(zz, yy, c), h, 3).wait_send()
            if h == 1:

                @pl.when(buddy_z != zz)
                def _():
                    send(held, h, 2).wait_send()

            else:
                send(held, h, 2).wait_send()

            @pl.when((zz >= z) & (z > 0))
            def _():
                send(held, h, 0).wait_send()

            @pl.when((zz <= z) & (z < lines - 1))
            def _():
                send(held, h, 1).wait_send()

    send(across, 1, 4).wait_send()
    own.wait()


def gather_blocks(obs_features, tile_count):
    rows, feat = obs_features.shape
    small = jax.ShapeDtypeStruct((1, feat), jnp.float32)
    vmem = pl.BlockSpec(memory_space=pltpu.VMEM)
    return pl.pallas_call(
        functools.partial(gather_kernel, tile_count // 4),
        out_shape=(
            jax.ShapeDtypeStruct((tile_count * rows, feat), obs_features.dtype),
            small,
            small,
        ),
        in_specs=[vmem],
        out_specs=(pl.BlockSpec(memory_space=pl.ANY), vmem, vmem),
        scratch_shapes=[
            pltpu.VMEM((8, feat), jnp.float32),
            pltpu.VMEM((tile_count, 8, feat), jnp.float32),
            pltpu.SemaphoreType.DMA((5, 2 * tile_count)),
            pltpu.SemaphoreType.DMA((2 * tile_count,)),
            pltpu.SemaphoreType.DMA((tile_count,)),
            pltpu.SemaphoreType.DMA((tile_count,)),
            pltpu.SemaphoreType.DMA,
        ],
        compiler_params=pltpu.CompilerParams(collective_id=0, has_side_effects=True),
    )(obs_features)


def scatter_kernel(count, order_ref, encoded_ref, out_ref, arrived, sends, recvs):
    me = lax.axis_index("tile")
    tile_local = encoded_ref.shape[1]
    greet_all(me, count)

    def copy(source, peer, k):
        return pltpu.make_async_remote_copy(
            src_ref=encoded_ref.at[peer],
            dst_ref=arrived.at[pl.ds(source * tile_local, tile_local)],
            send_sem=sends.at[k],
            recv_sem=recvs.at[source],
            device_id={"tile": peer},
            device_id_type=MESH,
        )

    def start(k, carry):
        copy(me, lax.rem(me + k, count), k).start()
        return carry

    def finish(k, carry):
        peer = lax.rem(me + k, count)
        copy(peer, peer, k).wait_send()
        copy(peer, peer, k).wait_recv()
        return carry

    lax.fori_loop(1, count, start, 0)
    arrived[pl.ds(me * tile_local, tile_local)] = encoded_ref[me]
    lax.fori_loop(1, count, finish, 0)

    def arrange(j, carry):
        out_ref[pl.ds(j, 1)] = arrived[pl.ds(order_ref[j], 1)]
        return carry

    lax.fori_loop(0, count * tile_local, arrange, 0, unroll=8)


def scatter(encoded, proc_order):
    count, tile_local, piece, width = encoded.shape
    vmem = pl.BlockSpec(memory_space=pltpu.VMEM)
    shape = (count * tile_local, piece, width)
    return pl.pallas_call(
        functools.partial(scatter_kernel, count),
        out_shape=jax.ShapeDtypeStruct(shape, encoded.dtype),
        in_specs=[pl.BlockSpec(memory_space=pltpu.SMEM), vmem],
        out_specs=vmem,
        scratch_shapes=[
            pltpu.VMEM(shape, encoded.dtype),
            pltpu.SemaphoreType.DMA((count,)),
            pltpu.SemaphoreType.DMA((count,)),
        ],
        compiler_params=pltpu.CompilerParams(collective_id=1, has_side_effects=True),
    )(proc_order, encoded).reshape(count * tile_local * piece, width)


def exchange(obs_features, block_lists, block_counts, block_position, tile_count, own_index):
    obs_blocks = obs_features.shape[0] // BLOCK
    tile_local = block_lists.shape[0] // tile_count
    entry_count = tile_local * NSEL
    capacity = max(2, 2 * entry_count // tile_count)
    spots = jnp.take(block_position, block_lists, axis=0)
    is_valid = jnp.arange(NSEL, dtype=jnp.int32)[None, :] < block_counts[:, None]
    owner_dev = (spots // obs_blocks).reshape(tile_count, entry_count)
    local_blk = (spots % obs_blocks).reshape(tile_count, entry_count)
    valid_rows = is_valid.reshape(tile_count, entry_count)
    entry_order = jnp.arange(entry_count, dtype=jnp.int32)
    earlier = (
        (owner_dev[:, :, None] == owner_dev[:, None, :])
        & valid_rows[:, None, :]
        & (entry_order[None, :] < entry_order[:, None])[None, :, :]
    )
    slot_rank = jnp.sum(earlier.astype(jnp.int32), axis=2)
    mine = valid_rows & (owner_dev == own_index)
    slot_ids = jnp.arange(capacity, dtype=jnp.int32)
    hits = mine[:, None, :] & (slot_rank[:, None, :] == slot_ids[None, :, None])
    slot_block = jnp.sum(jnp.where(hits, local_blk[:, None, :], 0), axis=2)
    my_owner = lax.dynamic_index_in_dim(owner_dev, own_index, 0, keepdims=False)
    my_rank = lax.dynamic_index_in_dim(slot_rank, own_index, 0, keepdims=False)
    my_valid = lax.dynamic_index_in_dim(valid_rows, own_index, 0, keepdims=False)
    pick = jnp.where(my_valid, my_owner * capacity + my_rank, 0)
    raw_blocks = obs_features.reshape(obs_blocks, BLOCK, obs_features.shape[1])
    incoming = lax.all_to_all(
        jnp.take(raw_blocks, slot_block, axis=0), "tile", split_axis=0, concat_axis=0, tiled=True
    )
    return incoming.reshape(tile_count * capacity * BLOCK, obs_features.shape[1]), pick


def local(
    grid_tokens,
    obs_features,
    w_obs,
    b_obs,
    w_query,
    w_key,
    w_value,
    w_out,
    block_lists,
    block_counts,
    block_position,
    proc_order,
):
    tile_count = lax.axis_size("tile")
    own_index = lax.axis_index("tile")
    tile_local = grid_tokens.shape[0] // TILE_ROWS
    width = grid_tokens.shape[1]
    near = tile_count <= 16 and tile_count % 8 == 0
    if near:
        blocks, feat_mean, feat_rstd = gather_blocks(obs_features, tile_count)
        lists, counts, position = block_lists, block_counts, block_position
    else:
        obs_wide = obs_features.astype(jnp.float32)
        first_sum, second_sum = lax.psum(
            (
                jnp.sum(obs_wide, axis=0, keepdims=True),
                jnp.sum(obs_wide * obs_wide, axis=0, keepdims=True),
            ),
            "tile",
        )
        obs_total = obs_features.shape[0] * tile_count
        feat_mean = first_sum / obs_total
        feat_rstd = lax.rsqrt(second_sum / obs_total - feat_mean * feat_mean + 1e-05)
        blocks, pick = exchange(
            obs_features, block_lists, block_counts, block_position, tile_count, own_index
        )
        lists = pick.reshape(tile_local, NSEL)
        counts = lax.dynamic_slice_in_dim(block_counts, own_index * tile_local, tile_local)
        position = jnp.arange(blocks.shape[0] // BLOCK, dtype=jnp.int32)
    encoded = attend(
        tile_count if near else 1,
        near,
        lists,
        counts,
        position,
        grid_tokens,
        blocks,
        feat_mean,
        feat_rstd,
        w_obs,
        b_obs,
        w_query,
        w_key,
        w_value,
        w_out,
    )
    if near:
        return scatter(encoded, proc_order)
    outgoing = encoded.reshape(tile_local, tile_count, TILE_ROWS // tile_count, width)
    arrived = lax.all_to_all(outgoing, "tile", split_axis=1, concat_axis=0, tiled=True)
    arrived = arrived.reshape(tile_count * tile_local, TILE_ROWS // tile_count, width)
    return jnp.take(arrived, proc_order, axis=0).reshape(
        tile_count * tile_local * (TILE_ROWS // tile_count), width
    )


def solution(mesh):
    in_specs = (
        P(("groups", "tile"), None),
        P(("groups", "tile"), None),
        P(),
        P(),
        P(),
        P(),
        P(),
        P(),
        P("groups", None),
        P("groups"),
        P("groups"),
        P("groups"),
    )
    out_specs = P(("groups", "tile"), None)
    return jax.shard_map(local, mesh=mesh, in_specs=in_specs, out_specs=out_specs, check_vma=False)
```

profile of v0, /device:TPU:13, one launch (start us, length us, event | category | flops | bytes accessed | tf_op | source)
XLA Modules:
  0.0 113.3 jit_solution(1031905631575381177)
XLA Ops:
  0.0 1.4 %copy.13.list_ref = s32[64,32]{1,0:T(8,128)} copy(s32[64,32]{0,1:T(8,128)} %param.20) | data formatting | bytes 16384 | tf_op args[8]
  1.4 50.8 %shard_map.118 = (bf16[32768,128]{1,0:T(8,128)(2,1)}, f32[1,128]{1,0:T(1,128)}, f32[1,128]{1,0:T(1,128)}) custom-call(bf16[2048,128]{1,0:T(8,128)(2,1)} %obs_ref.1), custom_call_target="tpu_custom_call" | custom-call | tf_op jit(solution)/shard_map/pallas_call | solution.py:393
  52.2 33.8 %shard_map.119.encoded_ref = bf16[16,4,8,512]{3,2,1,0:T(8,128)(2,1)} custom-call(s32[64,32]{1,0:T(8,128)} %copy.13.list_ref, s32[64]{0:T(128)} %count_ref.1, s32[512]{0:T(512)} %position_ref.1, bf16[512,512]{1,0:T(8,128)(2,1)} %grid_ref.1, bf16[32768,128]{1,0:T(8,128)(2,1)} %get-tuple-element.8.blocks_ref, f32[1,128]{1,0:T(1,128)} %get-tuple-element.9.mean_ref, ...), custom_call_target="tpu_custom_call" | custom-call | flops 12000000000 | bytes 6000000 | tf_op jit(solution)/shard_map/pallas_call | solution.py:153
  86.1 25.4 %shard_map.120 = bf16[64,8,512]{2,1,0:T(8,128)(2,1)} custom-call(s32[64]{0:T(128)} %order_ref.1, bf16[16,4,8,512]{3,2,1,0:T(8,128)(2,1)} %shard_map.119.encoded_ref), custom_call_target="tpu_custom_call" | custom-call | tf_op jit(solution)/shard_map/pallas_call | solution.py:455
  111.4 1.9 %copy.15 = bf16[512,512]{1,0:T(8,128)(2,1)} copy(bf16[512,512]{1,0:T(8,128)(2,1)} %bitcast.2) | data formatting | bytes 1048576
where the time goes:
time: 114 us; the launch traced here: 113 us
  Pallas kernels  110 us (96%)
  local copies, waits for them, and re-layouts  3.28 us (3%)
    pallas_call x1, Pallas kernels, gather_blocks(): pl.pallas_call(functools.partial(gather_kernel, tile_count // 4), out_sha...  50.8 us
    pallas_call x1, Pallas kernels, attend(): pl.pallas_call(functools.partial(attend_kernel, owned), grid_spec=pltpu.P...  33.8 us
    pallas_call x1, Pallas kernels, scatter(): pl.pallas_call(functools.partial(scatter_kernel, count), out_shape=jax.Sh...  25.4 us
    unnamed x2, local copies, waits for them, and re-layouts  3.28 us

commit v1 on v0

v1 whole, which is shorter than its diff:
```python
import functools

import jax
import jax.numpy as jnp
from jax import lax
from jax.experimental import pallas as pl
from jax.experimental.pallas import tpu as pltpu
from jax.sharding import PartitionSpec as P

HEADS = 8
BLOCK = 64
NSEL = 32
TILE_ROWS = 128
CHUNK = 512
NEG = -1e30


def attend_kernel(
    owned,
    list_ref,
    count_ref,
    position_ref,
    grid_ref,
    blocks_ref,
    mean_ref,
    rstd_ref,
    w_obs_ref,
    b_obs_ref,
    w_query_ref,
    w_key_ref,
    w_value_ref,
    w_out_ref,
    out_ref,
    raw,
    keys,
    values,
    copy_sem,
):
    tile = pl.program_id(0)
    tiles = pl.num_programs(0)
    key_span = NSEL * BLOCK
    width = grid_ref.shape[1]
    pair = 2 * (width // HEADS)
    base = lax.axis_index("tile") * tiles if owned else 0

    def fetch(which):
        slot = lax.rem(which, 2)

        def one(j, carry):
            spot = position_ref[list_ref[base + which, j]]
            pltpu.make_async_copy(
                blocks_ref.at[pl.ds(spot * BLOCK, BLOCK), :],
                raw.at[slot, pl.ds(j * BLOCK, BLOCK), :],
                copy_sem.at[slot],
            ).start()
            return carry

        lax.fori_loop(0, NSEL, one, 0)

    @pl.when(tile == 0)
    def _():
        fetch(tile)

    slot = lax.rem(tile, 2)
    pltpu.make_async_copy(
        blocks_ref.at[pl.ds(0, key_span), :], raw.at[slot], copy_sem.at[slot]
    ).wait()

    @pl.when(tile + 1 < tiles)
    def _():
        fetch(tile + 1)

    for start in range(0, key_span, CHUNK):
        rows = pl.ds(start, CHUNK)
        feats = raw[slot, rows, :].astype(jnp.float32)
        normed = ((feats - mean_ref[...]) * rstd_ref[...]).astype(jnp.bfloat16)
        hidden = jnp.dot(normed, w_obs_ref[...], preferred_element_type=jnp.float32)
        hidden = hidden + b_obs_ref[...]
        embedded = jax.nn.gelu(hidden, approximate=True).astype(jnp.bfloat16)
        keys[rows, :] = jnp.dot(
            embedded, w_key_ref[...], preferred_element_type=jnp.float32
        ).astype(jnp.bfloat16)
        values[rows, :] = jnp.dot(
            embedded, w_value_ref[...], preferred_element_type=jnp.float32
        ).astype(jnp.bfloat16)

    queries = jnp.dot(
        grid_ref[...], w_query_ref[...], preferred_element_type=jnp.float32
    ).astype(jnp.bfloat16)
    queries = queries * jnp.bfloat16(1.0 / (width // HEADS) ** 0.5)
    certain = 3 * key_span // 4
    used = count_ref[base + tile] * BLOCK
    key_index = certain + lax.broadcasted_iota(jnp.int32, (1, key_span - certain), 1)
    bias = jnp.where(key_index < used, 0.0, NEG).astype(jnp.float32)
    lane = lax.broadcasted_iota(jnp.int32, (TILE_ROWS, pair), 1)
    first = lane < pair // 2
    zero = jnp.zeros((), jnp.bfloat16)
    parts = []
    for p in range(HEADS // 2):
        columns = slice(p * pair, (p + 1) * pair)
        q = queries[:, columns]
        both = jnp.concatenate([jnp.where(first, q, zero), jnp.where(first, zero, q)], axis=0)
        scores = lax.dot_general(
            both,
            keys[:, columns],
            (((1,), (1,)), ((), ())),
            preferred_element_type=jnp.float32,
        )
        scores = jnp.concatenate([scores[:, :certain], scores[:, certain:] + bias], axis=1)
        peak = jnp.max(scores, axis=-1, keepdims=True)
        expo = jnp.exp(scores - peak)
        totals = jnp.sum(expo, axis=-1, keepdims=True)
        mixed = jnp.dot(
            expo.astype(jnp.bfloat16), values[:, columns], preferred_element_type=jnp.float32
        )
        mixed = mixed / totals
        parts.append(
            jnp.where(first, mixed[:TILE_ROWS], mixed[TILE_ROWS:]).astype(jnp.bfloat16)
        )
    attended = jnp.concatenate(parts, axis=1)
    encoded = jnp.dot(
        attended, w_out_ref[...], preferred_element_type=jnp.float32
    ).astype(jnp.bfloat16)
    out_ref[...] = encoded.reshape(out_ref.shape)


def attend(
    tile_count,
    owned,
    lists,
    counts,
    position,
    grid_tokens,
    blocks,
    mean,
    rstd,
    w_obs,
    b_obs,
    w_query,
    w_key,
    w_value,
    w_out,
):
    rows, width = grid_tokens.shape
    piece = TILE_ROWS // tile_count
    feat = blocks.shape[1]
    key_span = NSEL * BLOCK

    def whole(shape):
        return pl.BlockSpec(shape, lambda t, *_: (0, 0))

    square = whole((width, width))
    return pl.pallas_call(
        functools.partial(attend_kernel, owned),
        grid_spec=pltpu.PrefetchScalarGridSpec(
            num_scalar_prefetch=3,
            grid=(rows // TILE_ROWS,),
            in_specs=[
                pl.BlockSpec((TILE_ROWS, width), lambda t, *_: (t, 0)),
                pl.BlockSpec(memory_space=pl.ANY),
                whole((1, feat)),
                whole((1, feat)),
                whole((feat, width)),
                whole((1, width)),
                square,
                square,
                square,
                square,
            ],
            out_specs=pl.BlockSpec((tile_count, 1, piece, width), lambda t, *_: (0, t, 0, 0)),
            scratch_shapes=[
                pltpu.VMEM((2, key_span, feat), jnp.bfloat16),
                pltpu.VMEM((key_span, width), jnp.bfloat16),
                pltpu.VMEM((key_span, width), jnp.bfloat16),
                pltpu.SemaphoreType.DMA((2,)),
            ],
        ),
        out_shape=jax.ShapeDtypeStruct(
            (tile_count, rows // TILE_ROWS, piece, width), jnp.bfloat16
        ),
        compiler_params=pltpu.CompilerParams(dimension_semantics=("arbitrary",)),
        cost_estimate=pl.CostEstimate(
            flops=12_000_000_000, bytes_accessed=6_000_000, transcendentals=12_000_000
        ),
    )(
        lists,
        counts,
        position,
        grid_tokens,
        blocks,
        mean,
        rstd,
        w_obs,
        b_obs[None],
        w_query,
        w_key,
        w_value,
        w_out,
    )


MESH = pl.DeviceIdType.MESH


def greet_all(me, count):
    barrier = pltpu.get_barrier_semaphore()

    def one(k, carry):
        peer = lax.rem(me + k, count)
        pl.semaphore_signal(barrier, inc=1, device_id={"tile": peer}, device_id_type=MESH)
        return carry

    lax.fori_loop(1, count, one, 0)
    pl.semaphore_wait(barrier, count - 1)


LINES = 4
SIDES = LINES * 4
HALVES = 2
FIRST = 10
SECOND = 14
STEP = 8


def reorder(k, z):
    m = z // 2
    zz = z + m * (LINES - 1 - 2 * z)
    kk = k + zz * (1 - k // 2) * (1 - 2 * k)
    return kk + m * (LINES - 1 - 2 * kk)


def distance(zs, z):
    m = z // 2
    zz = z + m * (LINES - 1 - 2 * z)
    ss = zs + m * (LINES - 1 - 2 * zs)
    return ss + zz * (1 - ss // 2) * (1 - 2 * ss)


def plan_entries(me, lists_ref, count_ref, position_ref, plan, tiles, obs_blocks):
    entries = tiles * NSEL
    z, y, c = me // 4, lax.rem(me // 2, 2), lax.rem(me, 2)
    shift = obs_blocks.bit_length() - 1
    lane = lax.broadcasted_iota(jnp.int32, lists_ref.shape, 1)
    row = lax.broadcasted_iota(jnp.int32, (NSEL, 1), 0)
    ids, used = [], []
    for t in range(tiles):
        tile = me * tiles + t
        ids.append(jnp.sum(jnp.where(lane == tile, lists_ref[...], 0), axis=1, keepdims=True))
        used.append((row < count_ref[tile]).astype(jnp.int32))
    ids = jnp.concatenate(ids, axis=0)
    used = jnp.concatenate(used, axis=0)
    blocks = position_ref.shape[1]
    which = lax.broadcasted_iota(jnp.int32, (entries, blocks), 1)
    spot = jnp.sum(jnp.where(ids == which, position_ref[...], 0), axis=1, keepdims=True)
    owner = lax.shift_right_logical(spot, shift)
    inner = spot & (obs_blocks - 1)
    oz = lax.shift_right_logical(owner, 2)
    oy = lax.shift_right_logical(owner, 1) & 1
    near = jnp.zeros_like(oz)
    for zs in range(LINES):
        near = jnp.where(oz == zs, distance(zs, z), near)
    slot = near * 4 + (oy ^ y) * 2 + ((owner & 1) ^ c)
    slot = slot * used
    address = (slot * obs_blocks + inner) * used
    entry = lax.broadcasted_iota(jnp.int32, (entries, 1), 0)
    key = slot * entries + entry
    across = lax.broadcasted_iota(jnp.int32, (entries, entries), 1)
    down = lax.broadcasted_iota(jnp.int32, (entries, entries), 0)
    key_row = jnp.sum(jnp.where(across == down, key, 0), axis=0, keepdims=True)
    rank_row = jnp.sum((key < key_row).astype(jnp.int32), axis=0, keepdims=True)
    rank = jnp.sum((key_row < key).astype(jnp.int32), axis=1, keepdims=True)
    sorted_row = jnp.sum(jnp.where(rank == across, address, 0), axis=0, keepdims=True)
    plan[0:1, :] = rank_row
    plan[1:2, :] = sorted_row
    plan[2:3, :] = jnp.minimum(sorted_row, FIRST * obs_blocks - 1)
    behind = sorted_row - FIRST * obs_blocks
    plan[3:4, :] = jnp.minimum(jnp.maximum(behind, 0), (SECOND - FIRST) * obs_blocks - 1)


def fused_kernel(
    lists_ref,
    count_ref,
    position_ref,
    order_ref,
    grid_ref,
    obs_ref,
    w_obs_ref,
    b_obs_ref,
    w_query_ref,
    w_key_ref,
    w_value_ref,
    w_out_ref,
    out_ref,
    land,
    early,
    later,
    feed,
    keys,
    values,
    queries,
    encoded,
    arrived,
    plan,
    plan_s,
    part,
    parts,
    stats,
    sends,
    recvs,
    part_sends,
    part_recvs,
    out_sends,
    out_recvs,
    own_sems,
    stage_sems,
    plan_sem,
):
    count = SIDES
    me = lax.axis_index("tile")
    z, y, c = me // 4, lax.rem(me // 2, 2), lax.rem(me, 2)
    rows = obs_ref.shape[0]
    half = rows // HALVES
    tokens, width = grid_ref.shape
    tiles = tokens // TILE_ROWS
    obs_blocks = rows
    pair = 2 * (width // HEADS)
    order = [reorder(k, z) for k in range(LINES)]

    def index(zz, yy, cc):
        return (zz * 2 + yy) * 2 + cc

    def slot_of(zs, ys, cs, zt, yt, ct):
        dy = lax.rem(ys + yt, 2)
        dc = lax.rem(cs + ct, 2)
        return distance(zs, zt) * 4 + dy * 2 + dc

    def span(slot, h):
        return pl.ds(pl.multiple_of(slot * rows + h * half, half), half)

    def send(source, target, h, way, own=False):
        slot = slot_of(*source, *target)
        held = slot_of(*source, z, y, c)
        block = index(*source)
        return pltpu.make_async_remote_copy(
            src_ref=obs_ref.at[pl.ds(h * half, half)] if own else land.at[span(held, h)],
            dst_ref=land.at[span(slot, h)],
            send_sem=sends.at[way, HALVES * block + h],
            recv_sem=recvs.at[HALVES * block + h],
            device_id={"tile": index(*target)},
            device_id_type=MESH,
        )

    mine = (z, y, c)
    across = (z, 1 - y, c)
    beside = (z, y, 1 - c)
    started = []

    def launch(source, target, h, way, own=False, when=None):
        def issue(finish):
            def go():
                copy = send(source(), target(), h, way, own)
                copy.wait_send() if finish else copy.start()

            if when is None:
                go()
            else:
                pl.when(when())(go)

        started.append(issue)
        issue(False)

    def below_me():
        return z - 1, y, c

    def above_me():
        return z + 1, y, c

    def held_by_me():
        return mine

    def to_across():
        return across

    def to_beside():
        return beside

    def arrive(source, h):
        send(source, beside, h, 3).wait_recv()

    greet_all(me, count)
    for h in range(HALVES):
        launch(held_by_me, below_me, h, 0, True, lambda: z > 0)
        launch(held_by_me, above_me, h, 1, True, lambda: z < LINES - 1)
        launch(held_by_me, to_across, h, 2, True)
        launch(held_by_me, to_beside, h, 3, True)
    own_copies = [
        pltpu.make_async_copy(obs_ref, ref.at[pl.ds(0, rows)], own_sems.at[i])
        for i, ref in enumerate((land, early))
    ]
    for copy in own_copies:
        copy.start()

    feats = obs_ref[...].reshape(rows * BLOCK, obs_ref.shape[2]).astype(jnp.float32)
    part[...] = jnp.zeros_like(part)
    part[0:1, :] = jnp.sum(feats, axis=0, keepdims=True)
    part[1:2, :] = jnp.sum(feats * feats, axis=0, keepdims=True)
    parts[pl.ds(me, 1)] = part[...][None]

    def share_copy(k, source, peer):
        return pltpu.make_async_remote_copy(
            src_ref=part,
            dst_ref=parts.at[source],
            send_sem=part_sends.at[k],
            recv_sem=part_recvs.at[source],
            device_id={"tile": peer},
            device_id_type=MESH,
        )

    def share(k, carry):
        share_copy(k, me, lax.rem(me + k, count)).start()
        return carry

    lax.fori_loop(1, count, share, 0)

    plan_entries(me, lists_ref, count_ref, position_ref, plan, tiles, obs_blocks)
    plan_copy = pltpu.make_async_copy(plan, plan_s, plan_sem)
    plan_copy.start()
    queries[...] = jnp.dot(
        grid_ref[...], w_query_ref[...], preferred_element_type=jnp.float32
    ).astype(jnp.bfloat16) * jnp.bfloat16(1.0 / (width // HEADS) ** 0.5)
    plan_copy.wait()

    def column(k, h):
        def source():
            return order[k], y, c

        arrive(source(), h)
        launch(source, below_me, h, 0, False, lambda: (order[k] > z) & (z > 0))
        launch(source, above_me, h, 1, False, lambda: (order[k] < z) & (z < LINES - 1))
        if not (k == 1 and h == 1):
            launch(source, to_across, h, 2)
        launch(source, to_beside, h, 3)

    def opposite(k, h):
        def source():
            return order[k], 1 - y, c

        arrive(source(), h)
        if k == 0 and h == 1:
            launch(source, lambda: (order[1], y, c), h, 4)
        launch(source, to_beside, h, 3)

    def twin(k, dy, h):
        arrive((order[k], lax.rem(y + dy, 2), 1 - c), h)

    def stage(ref, sem, low, first, last):
        return pltpu.make_async_copy(
            land.at[pl.ds(first * rows, (last - first) * rows)],
            ref.at[pl.ds((first - low) * rows, (last - first) * rows)],
            stage_sems.at[sem],
        )

    for h in range(HALVES):
        column(1, h)
        opposite(0, h)
    for h in range(HALVES):
        twin(0, 0, h)
        twin(0, 1, h)
    stage(early, 0, 0, 1, 4).start()
    for h in range(HALVES):
        column(2, h)
        opposite(1, h)
    for h in range(HALVES):
        twin(1, 0, h)
    stage(early, 1, 0, 4, 6).start()
    for h in range(HALVES):
        twin(1, 1, h)
        twin(2, 0, h)
    stage(early, 2, 0, 6, FIRST).start()

    def gathered(k, carry):
        peer = lax.rem(me + k, count)
        share_copy(k, peer, peer).wait_send()
        share_copy(k, peer, peer).wait_recv()
        return carry

    lax.fori_loop(1, count, gathered, 0)
    sums = jnp.sum(parts[...], axis=0)
    total = rows * BLOCK * count
    mean = sums[0:1, :] / total
    stats[0:1, :] = mean
    stats[1:2, :] = lax.rsqrt(sums[1:2, :] / total - mean * mean + 1e-05)

    for copy in own_copies:
        copy.wait()
    stage(early, 0, 0, 1, 4).wait()
    stage(early, 1, 0, 4, 6).wait()
    stage(early, 2, 0, 6, FIRST).wait()

    chunk_rows = STEP * BLOCK
    chunks = tiles * NSEL // STEP
    share_of = chunks // 8

    def chunk(i, carry):
        @pl.when(i == share_of - 1)
        def _():
            column(3, 0)

        @pl.when(i == share_of)
        def _():
            opposite(2, 0)

        @pl.when(i == 2 * share_of - 1)
        def _():
            column(3, 1)

        @pl.when(i == 2 * share_of)
        def _():
            opposite(2, 1)
            for h in range(HALVES):
                twin(2, 1, h)
                twin(3, 0, h)
            stage(later, 3, FIRST, FIRST, SECOND).start()
            stage(later, 3, FIRST, FIRST, SECOND).wait()

        @pl.when(i == 4 * share_of)
        def _():
            opposite(3, 0)

        @pl.when(i == 5 * share_of)
        def _():
            opposite(3, 1)

        @pl.when(i == 6 * share_of)
        def _():
            for h in range(HALVES):
                twin(3, 1, h)

        @pl.when(i < 2 * share_of)
        def _():
            for u in range(STEP):
                feed[u] = early[plan_s[2, i * STEP + u]]

        @pl.when((i >= 2 * share_of) & (i < 6 * share_of))
        def _():
            for u in range(STEP):
                n = i * STEP + u
                spot = jnp.full(feed.shape[1:], plan_s[1, n], jnp.int32)
                feed[u] = jnp.where(
                    spot < FIRST * obs_blocks, early[plan_s[2, n]], later[plan_s[3, n]]
                )

        @pl.when(i >= 6 * share_of)
        def _():
            for u in range(STEP):
                feed[u] = land[plan_s[1, i * STEP + u]]

        feats = feed[...].reshape(chunk_rows, feed.shape[2]).astype(jnp.float32)
        normed = ((feats - stats[0:1, :]) * stats[1:2, :]).astype(jnp.bfloat16)
        hidden = jnp.dot(normed, w_obs_ref[...], preferred_element_type=jnp.float32)
        hidden = hidden + b_obs_ref[...]
        embedded = jax.nn.gelu(hidden, approximate=True).astype(jnp.bfloat16)
        place = pl.ds(i * STEP, STEP)
        key_rows = jnp.dot(embedded, w_key_ref[...], preferred_element_type=jnp.float32)
        keys[place] = key_rows.astype(jnp.bfloat16).reshape(STEP, BLOCK, width)
        value_rows = jnp.dot(embedded, w_value_ref[...], preferred_element_type=jnp.float32)
        values[place] = value_rows.astype(jnp.bfloat16).reshape(STEP, BLOCK, width)
        return carry

    lax.fori_loop(0, chunks, chunk, 0)

    key_span = NSEL * BLOCK
    certain = 3 * key_span // 4
    first = lax.broadcasted_iota(jnp.int32, (TILE_ROWS, pair), 1) < pair // 2
    zero = jnp.zeros((), jnp.bfloat16)
    piece = TILE_ROWS // count

    def out_copy(t, source, peer, k):
        return pltpu.make_async_remote_copy(
            src_ref=encoded.at[t, peer],
            dst_ref=arrived.at[source * tiles + t],
            send_sem=out_sends.at[t * count + k],
            recv_sem=out_recvs.at[source * tiles + t],
            device_id={"tile": peer},
            device_id_type=MESH,
        )

    def attend_tile(t, carry):
        used = count_ref[me * tiles + t] * BLOCK
        key_index = certain + lax.broadcasted_iota(jnp.int32, (1, key_span - certain), 1)
        bias = jnp.where(key_index < used, 0.0, NEG).astype(jnp.float32)
        places = [plan_s[0, t * NSEL + j] for j in range(NSEL)]
        outs = []
        for p in range(HEADS // 2):
            columns = slice(p * pair, (p + 1) * pair)
            q = queries[pl.ds(pl.multiple_of(t * TILE_ROWS, TILE_ROWS), TILE_ROWS), columns]
            both = jnp.concatenate([jnp.where(first, q, zero), jnp.where(first, zero, q)], axis=0)
            key_rows = jnp.concatenate([keys[place, :, columns] for place in places], axis=0)
            value_rows = jnp.concatenate([values[place, :, columns] for place in places], axis=0)
            scores = lax.dot_general(
                both, key_rows, (((1,), (1,)), ((), ())), preferred_element_type=jnp.float32
            )
            scores = jnp.concatenate([scores[:, :certain], scores[:, certain:] + bias], axis=1)
            peak = jnp.max(scores, axis=-1, keepdims=True)
            expo = jnp.exp(scores - peak)
            totals = jnp.sum(expo, axis=-1, keepdims=True)
            mixed = jnp.dot(
                expo.astype(jnp.bfloat16), value_rows, preferred_element_type=jnp.float32
            )
            mixed = mixed / totals
            outs.append(jnp.where(first, mixed[:TILE_ROWS], mixed[TILE_ROWS:]).astype(jnp.bfloat16))
        attended = jnp.concatenate(outs, axis=1)
        result = jnp.dot(attended, w_out_ref[...], preferred_element_type=jnp.float32)
        encoded[t] = result.astype(jnp.bfloat16).reshape(count, piece, width)

        def start(k, carry):
            out_copy(t, me, lax.rem(me + k, count), k).start()
            return carry

        lax.fori_loop(1, count, start, 0)
        arrived[pl.ds(me * tiles + t, 1)] = encoded[t, pl.ds(me, 1)]
        return carry

    lax.fori_loop(0, tiles, attend_tile, 0)

    for issue in started:
        issue(True)

    def finish(n, carry):
        t, k = n // (count - 1), 1 + lax.rem(n, count - 1)
        peer = lax.rem(me + k, count)
        out_copy(t, peer, peer, k).wait_send()
        out_copy(t, peer, peer, k).wait_recv()
        return carry

    lax.fori_loop(0, tiles * (count - 1), finish, 0)

    def arrange(j, carry):
        out_ref[pl.ds(j, 1)] = arrived[pl.ds(order_ref[j], 1)]
        return carry

    lax.fori_loop(0, count * tiles, arrange, 0, unroll=8)


def fused(lists, counts, position, proc_order, grid_tokens, obs_features, w_obs, b_obs, w_query, w_key, w_value, w_out):
    tokens, width = grid_tokens.shape
    rows, feat = obs_features.shape[0] // BLOCK, obs_features.shape[1]
    tiles = tokens // TILE_ROWS
    count = SIDES
    piece = TILE_ROWS // count
    entries = tiles * NSEL
    shape = (count * tiles, piece, width)
    vmem = pl.BlockSpec(memory_space=pltpu.VMEM)
    smem = pl.BlockSpec(memory_space=pltpu.SMEM)
    bf16 = jnp.bfloat16
    dma = pltpu.SemaphoreType.DMA
    return pl.pallas_call(
        fused_kernel,
        out_shape=jax.ShapeDtypeStruct(shape, bf16),
        in_specs=[vmem, smem, vmem, smem] + [vmem] * 8,
        out_specs=vmem,
        scratch_shapes=[
            pltpu.VMEM((SIDES * rows, BLOCK, feat), bf16),
            pltpu.VMEM((FIRST * rows, BLOCK, feat), bf16),
            pltpu.VMEM(((SECOND - FIRST) * rows, BLOCK, feat), bf16),
            pltpu.VMEM((STEP, BLOCK, feat), bf16),
            pltpu.VMEM((entries, BLOCK, width), bf16),
            pltpu.VMEM((entries, BLOCK, width), bf16),
            pltpu.VMEM((tokens, width), bf16),
            pltpu.VMEM((tiles, count, piece, width), bf16),
            pltpu.VMEM(shape, bf16),
            pltpu.VMEM((8, entries), jnp.int32),
            pltpu.SMEM((8, entries), jnp.int32),
            pltpu.VMEM((8, feat), jnp.float32),
            pltpu.VMEM((count, 8, feat), jnp.float32),
            pltpu.VMEM((8, feat), jnp.float32),
            dma((5, HALVES * count)),
            dma((HALVES * count,)),
            dma((count,)),
            dma((count,)),
            dma((tiles * count,)),
            dma((tiles * count,)),
            dma((2,)),
            dma((4,)),
            dma,
        ],
        compiler_params=pltpu.CompilerParams(
            collective_id=0, has_side_effects=True, vmem_limit_bytes=62 * 2**20
        ),
    )(
        lists.T,
        counts,
        position[None],
        proc_order,
        grid_tokens,
        obs_features.reshape(rows, BLOCK, feat),
        w_obs,
        b_obs[None],
        w_query,
        w_key,
        w_value,
        w_out,
    ).reshape(count * tiles * piece, width)


def exchange(obs_features, block_lists, block_counts, block_position, tile_count, own_index):
    obs_blocks = obs_features.shape[0] // BLOCK
    tile_local = block_lists.shape[0] // tile_count
    entry_count = tile_local * NSEL
    capacity = max(2, 2 * entry_count // tile_count)
    spots = jnp.take(block_position, block_lists, axis=0)
    is_valid = jnp.arange(NSEL, dtype=jnp.int32)[None, :] < block_counts[:, None]
    owner_dev = (spots // obs_blocks).reshape(tile_count, entry_count)
    local_blk = (spots % obs_blocks).reshape(tile_count, entry_count)
    valid_rows = is_valid.reshape(tile_count, entry_count)
    entry_order = jnp.arange(entry_count, dtype=jnp.int32)
    earlier = (
        (owner_dev[:, :, None] == owner_dev[:, None, :])
        & valid_rows[:, None, :]
        & (entry_order[None, :] < entry_order[:, None])[None, :, :]
    )
    slot_rank = jnp.sum(earlier.astype(jnp.int32), axis=2)
    mine = valid_rows & (owner_dev == own_index)
    slot_ids = jnp.arange(capacity, dtype=jnp.int32)
    hits = mine[:, None, :] & (slot_rank[:, None, :] == slot_ids[None, :, None])
    slot_block = jnp.sum(jnp.where(hits, local_blk[:, None, :], 0), axis=2)
    my_owner = lax.dynamic_index_in_dim(owner_dev, own_index, 0, keepdims=False)
    my_rank = lax.dynamic_index_in_dim(slot_rank, own_index, 0, keepdims=False)
    my_valid = lax.dynamic_index_in_dim(valid_rows, own_index, 0, keepdims=False)
    pick = jnp.where(my_valid, my_owner * capacity + my_rank, 0)
    raw_blocks = obs_features.reshape(obs_blocks, BLOCK, obs_features.shape[1])
    chosen = slot_block.reshape(-1, 1) == jnp.arange(obs_blocks, dtype=jnp.int32)[None, :]
    outgoing = jnp.einsum(
        "sb,brf->srf",
        chosen.astype(raw_blocks.dtype),
        raw_blocks,
        preferred_element_type=jnp.float32,
    ).astype(raw_blocks.dtype)
    incoming = lax.all_to_all(outgoing, "tile", split_axis=0, concat_axis=0, tiled=True)
    return incoming.reshape(tile_count * capacity * BLOCK, obs_features.shape[1]), pick


def local(
    grid_tokens,
    obs_features,
    w_obs,
    b_obs,
    w_query,
    w_key,
    w_value,
    w_out,
    block_lists,
    block_counts,
    block_position,
    proc_order,
):
    tile_count = lax.axis_size("tile")
    own_index = lax.axis_index("tile")
    tile_local = grid_tokens.shape[0] // TILE_ROWS
    width = grid_tokens.shape[1]
    if tile_count == SIDES:
        return fused(
            block_lists,
            block_counts,
            block_position,
            proc_order,
            grid_tokens,
            obs_features,
            w_obs,
            b_obs,
            w_query,
            w_key,
            w_value,
            w_out,
        )
    obs_wide = obs_features.astype(jnp.float32)
    first_sum, second_sum = lax.psum(
        (
            jnp.sum(obs_wide, axis=0, keepdims=True),
            jnp.sum(obs_wide * obs_wide, axis=0, keepdims=True),
        ),
        "tile",
    )
    obs_total = obs_features.shape[0] * tile_count
    feat_mean = first_sum / obs_total
    feat_rstd = lax.rsqrt(second_sum / obs_total - feat_mean * feat_mean + 1e-05)
    blocks, pick = exchange(
        obs_features, block_lists, block_counts, block_position, tile_count, own_index
    )
    encoded = attend(
        1,
        False,
        pick.reshape(tile_local, NSEL),
        lax.dynamic_slice_in_dim(block_counts, own_index * tile_local, tile_local),
        jnp.arange(blocks.shape[0] // BLOCK, dtype=jnp.int32),
        grid_tokens,
        blocks,
        feat_mean,
        feat_rstd,
        w_obs,
        b_obs,
        w_query,
        w_key,
        w_value,
        w_out,
    )
    outgoing = encoded.reshape(tile_local, tile_count, TILE_ROWS // tile_count, width)
    arrived = lax.all_to_all(outgoing, "tile", split_axis=1, concat_axis=0, tiled=True)
    arrived = arrived.reshape(tile_count * tile_local, TILE_ROWS // tile_count, width)
    return jnp.take(arrived, proc_order, axis=0).reshape(
        tile_count * tile_local * (TILE_ROWS // tile_count), width
    )


def solution(mesh):
    in_specs = (
        P(("groups", "tile"), None),
        P(("groups", "tile"), None),
        P(),
        P(),
        P(),
        P(),
        P(),
        P(),
        P("groups", None),
        P("groups"),
        P("groups"),
        P("groups"),
    )
    out_specs = P(("groups", "tile"), None)
    return jax.shard_map(local, mesh=mesh, in_specs=in_specs, out_specs=out_specs, check_vma=False)
```

time: 114 us -> 91 us (0.80)
  the two profiles are of different devices: /device:TPU:13 before, /device:TPU:0 now
where the time goes in v1:
time: 91 us; the launch traced here: 90.9 us
  Pallas kernels  89 us (98%)
  local copies, waits for them, and re-layouts  1.87 us (2%)
    pallas_call x1, Pallas kernels, fused(): pl.pallas_call(fused_kernel, out_shape=jax.ShapeDtypeStruct(shape, bf16),...  89 us
    unnamed x1, local copies, waits for them, and re-layouts  1.87 us

profile of v1, /device:TPU:0, one launch (start us, length us, event | category | flops | bytes accessed | tf_op | source)
XLA Modules:
  0.0 90.9 jit_solution(2411520215623208991)
XLA Ops:
  0.0 89.0 %shard_map.118 = bf16[64,8,512]{2,1,0:T(8,128)(2,1)} custom-call(s32[32,64]{1,0:T(8,128)} %bitcast.7, s32[64]{0:T(128)} %count_ref.1, s32[1,512]{1,0:T(1,128)} %bitcast.8, s32[64]{0:T(128)} %order_ref.1, bf16[512,512]{1,0:T(8,128)(2,1)} %grid_ref.1, bf16[32,64,128]{2,1,0:T(8,128)(2,1)} %bitcast.6, bf16[128,512]{1,0:T(8,128)(2,1)} %w_obs_ref.1, ...), custom_call_target="tpu_custom_call" | custom-call | tf_op jit(solution)/shard_map/pallas_call | solution.py:657
  89.0 1.9 %copy.14 = bf16[512,512]{1,0:T(8,128)(2,1)} copy(bf16[512,512]{1,0:T(8,128)(2,1)} %bitcast.5) | data formatting | bytes 1048576

commit v2 on v1

--- a/solution.py
+++ b/solution.py
@@ -216,9 +216,8 @@
 
 LINES = 4
 SIDES = LINES * 4
-HALVES = 2
-FIRST = 10
-SECOND = 14
+CORES = 2
+PARTS = 1
 STEP = 8
 
 
@@ -238,7 +237,7 @@
 
 def plan_entries(me, lists_ref, count_ref, position_ref, plan, tiles, obs_blocks):
     entries = tiles * NSEL
-    z, y, c = me // 4, lax.rem(me // 2, 2), lax.rem(me, 2)
+    z, y = me // 4, lax.rem(me // 2, 2)
     shift = obs_blocks.bit_length() - 1
     lane = lax.broadcasted_iota(jnp.int32, lists_ref.shape, 1)
     row = lax.broadcasted_iota(jnp.int32, (NSEL, 1), 0)
@@ -259,11 +258,11 @@
     near = jnp.zeros_like(oz)
     for zs in range(LINES):
         near = jnp.where(oz == zs, distance(zs, z), near)
-    slot = near * 4 + (oy ^ y) * 2 + ((owner & 1) ^ c)
-    slot = slot * used
+    slot = near * 4 + (oy ^ y) * 2 + (owner & 1)
     address = (slot * obs_blocks + inner) * used
+    turn = jnp.where(slot == 7, 14, jnp.where((slot > 7) & (slot < 15), slot - 1, slot)) * used
     entry = lax.broadcasted_iota(jnp.int32, (entries, 1), 0)
-    key = slot * entries + entry
+    key = turn * entries + entry
     across = lax.broadcasted_iota(jnp.int32, (entries, entries), 1)
     down = lax.broadcasted_iota(jnp.int32, (entries, entries), 0)
     key_row = jnp.sum(jnp.where(across == down, key, 0), axis=0, keepdims=True)
@@ -272,9 +271,6 @@
     sorted_row = jnp.sum(jnp.where(rank == across, address, 0), axis=0, keepdims=True)
     plan[0:1, :] = rank_row
     plan[1:2, :] = sorted_row
-    plan[2:3, :] = jnp.minimum(sorted_row, FIRST * obs_blocks - 1)
-    behind = sorted_row - FIRST * obs_blocks
-    plan[3:4, :] = jnp.minimum(jnp.maximum(behind, 0), (SECOND - FIRST) * obs_blocks - 1)
 
 
 def fused_kernel(
@@ -282,19 +278,24 @@
     count_ref,
     position_ref,
     order_ref,
+    b_obs_ref,
+    obs_ref,
+    grid_hbm,
+    w_obs_hbm,
+    w_query_hbm,
+    w_key_hbm,
+    w_value_hbm,
+    w_out_hbm,
+    out_ref,
+    land,
+    ready,
+    feed,
     grid_ref,
-    obs_ref,
     w_obs_ref,
-    b_obs_ref,
     w_query_ref,
     w_key_ref,
     w_value_ref,
     w_out_ref,
-    out_ref,
-    land,
-    early,
-    later,
-    feed,
     keys,
     values,
     queries,
@@ -302,8 +303,8 @@
     arrived,
     plan,
     plan_s,
-    part,
-    parts,
+    tally,
+    tallies,
     stats,
     sends,
     recvs,
@@ -313,52 +314,72 @@
     out_recvs,
     own_sems,
     stage_sems,
+    load_sems,
     plan_sem,
 ):
     count = SIDES
     me = lax.axis_index("tile")
     z, y, c = me // 4, lax.rem(me // 2, 2), lax.rem(me, 2)
     rows = obs_ref.shape[0]
-    half = rows // HALVES
+    half = rows // CORES
+    bit = half // PARTS
     tokens, width = grid_ref.shape
     tiles = tokens // TILE_ROWS
     obs_blocks = rows
     pair = 2 * (width // HEADS)
     order = [reorder(k, z) for k in range(LINES)]
+    middle = (z > 0) & (z < LINES - 1)
+    edge = jnp.logical_not(middle)
+
+    loads = [
+        pltpu.make_async_copy(source, target, load_sems.at[i])
+        for i, (source, target) in enumerate(
+            (
+                (grid_hbm, grid_ref),
+                (w_query_hbm, w_query_ref),
+                (w_obs_hbm, w_obs_ref),
+                (w_key_hbm, w_key_ref),
+                (w_value_hbm, w_value_ref),
+                (w_out_hbm, w_out_ref),
+            )
+        )
+    ]
+    own_place = pl.ds(pl.multiple_of(c * rows, rows), rows)
+    own_copies = [
+        pltpu.make_async_copy(obs_ref, ref.at[own_place], own_sems.at[i])
+        for i, ref in enumerate((ready, land))
+    ]
 
     def index(zz, yy, cc):
         return (zz * 2 + yy) * 2 + cc
 
-    def slot_of(zs, ys, cs, zt, yt, ct):
-        dy = lax.rem(ys + yt, 2)
-        dc = lax.rem(cs + ct, 2)
-        return distance(zs, zt) * 4 + dy * 2 + dc
-
-    def span(slot, h):
-        return pl.ds(pl.multiple_of(slot * rows + h * half, half), half)
-
-    def send(source, target, h, way, own=False):
-        slot = slot_of(*source, *target)
-        held = slot_of(*source, z, y, c)
+    def slot_of(source, zt, yt):
+        zs, ys, cs = source
+        return distance(zs, zt) * 4 + lax.rem(ys + yt, 2) * 2 + cs
+
+    def span(slot, side, part):
+        return pl.ds(pl.multiple_of(slot * rows + side * half + part * bit, bit), bit)
+
+    def send(source, target, side, part, way, own=False):
         block = index(*source)
+        piece = (block * CORES + side) * PARTS + part
         return pltpu.make_async_remote_copy(
-            src_ref=obs_ref.at[pl.ds(h * half, half)] if own else land.at[span(held, h)],
-            dst_ref=land.at[span(slot, h)],
-            send_sem=sends.at[way, HALVES * block + h],
-            recv_sem=recvs.at[HALVES * block + h],
+            src_ref=obs_ref.at[pl.ds(pl.multiple_of(side * half + part * bit, bit), bit)]
+            if own
+            else land.at[span(slot_of(source, z, y), side, part)],
+            dst_ref=land.at[span(slot_of(source, target[0], target[1]), side, part)],
+            send_sem=sends.at[way, piece],
+            recv_sem=recvs.at[piece],
             device_id={"tile": index(*target)},
             device_id_type=MESH,
         )
 
-    mine = (z, y, c)
-    across = (z, 1 - y, c)
-    beside = (z, y, 1 - c)
     started = []
 
-    def launch(source, target, h, way, own=False, when=None):
+    def launch(source, target, side, part, way, own=False, when=None):
         def issue(finish):
             def go():
-                copy = send(source(), target(), h, way, own)
+                copy = send(source(), target(), side(), part, way, own)
                 copy.wait_send() if finish else copy.start()
 
             if when is None:
@@ -375,41 +396,65 @@
     def above_me():
         return z + 1, y, c
 
-    def held_by_me():
-        return mine
-
     def to_across():
-        return across
+        return z, 1 - y, c
 
     def to_beside():
-        return beside
-
-    def arrive(source, h):
-        send(source, beside, h, 3).wait_recv()
-
+        return z, y, 1 - c
+
+    def my_side():
+        return c
+
+    def other_side():
+        return 1 - c
+
+    def arrive(source, side, part):
+        send(source, to_beside(), side, part, 3).wait_recv()
+
+    def spread(source, own, when):
+        def both(cond):
+            return cond if when is None else lambda: when() & cond()
+
+        for part in range(PARTS):
+            launch(source, below_me, my_side, part, 0, own, both(lambda: z > 0))
+            launch(source, above_me, my_side, part, 1, own, both(lambda: z < LINES - 1))
+            launch(source, to_across, my_side, part, 2, own, when)
+
+    for copy in own_copies + loads:
+        copy.start()
     greet_all(me, count)
-    for h in range(HALVES):
-        launch(held_by_me, below_me, h, 0, True, lambda: z > 0)
-        launch(held_by_me, above_me, h, 1, True, lambda: z < LINES - 1)
-        launch(held_by_me, to_across, h, 2, True)
-        launch(held_by_me, to_beside, h, 3, True)
-    own_copies = [
-        pltpu.make_async_copy(obs_ref, ref.at[pl.ds(0, rows)], own_sems.at[i])
-        for i, ref in enumerate((land, early))
-    ]
-    for copy in own_copies:
-        copy.start()
-
-    feats = obs_ref[...].reshape(rows * BLOCK, obs_ref.shape[2]).astype(jnp.float32)
-    part[...] = jnp.zeros_like(part)
-    part[0:1, :] = jnp.sum(feats, axis=0, keepdims=True)
-    part[1:2, :] = jnp.sum(feats * feats, axis=0, keepdims=True)
-    parts[pl.ds(me, 1)] = part[...][None]
+    for part in range(PARTS):
+        launch(lambda: (z, y, c), to_beside, other_side, part, 3, True)
+    spread(lambda: (z, y, 0), True, lambda: c == 0)
+
+    @pl.when(c == 1)
+    def _():
+        for part in range(PARTS):
+            arrive((z, y, 0), c, part)
+
+    spread(lambda: (z, y, 0), False, lambda: c == 1)
+
+    @pl.when(c == 0)
+    def _():
+        for part in range(PARTS):
+            arrive((z, y, 1), c, part)
+
+    spread(lambda: (z, y, 1), False, lambda: c == 0)
+    spread(lambda: (z, y, 1), True, lambda: c == 1)
+    for part in range(PARTS):
+        launch(lambda: (z, y, c), to_beside, my_side, part, 3, True)
+
+    own_copies[0].wait()
+    feats = ready[own_place].reshape(rows * BLOCK, obs_ref.shape[2]).astype(jnp.float32)
+    tally[...] = jnp.zeros_like(tally)
+    tally[0:1, :] = jnp.sum(feats, axis=0, keepdims=True)
+    tally[1:2, :] = jnp.sum(feats * feats, axis=0, keepdims=True)
+    tallies[pl.ds(me, 1)] = tally[...][None]
 
     def share_copy(k, source, peer):
         return pltpu.make_async_remote_copy(
-            src_ref=part,
-            dst_ref=parts.at[source],
+            src_ref=tally,
+            dst_ref=tallies.at[source],
             send_sem=part_sends.at[k],
             recv_sem=part_recvs.at[source],
             device_id={"tile": peer},
@@ -425,58 +470,80 @@
     plan_entries(me, lists_ref, count_ref, position_ref, plan, tiles, obs_blocks)
     plan_copy = pltpu.make_async_copy(plan, plan_s, plan_sem)
     plan_copy.start()
+    loads[0].wait()
+    loads[1].wait()
     queries[...] = jnp.dot(
         grid_ref[...], w_query_ref[...], preferred_element_type=jnp.float32
     ).astype(jnp.bfloat16) * jnp.bfloat16(1.0 / (width // HEADS) ** 0.5)
     plan_copy.wait()
 
-    def column(k, h):
+    def column(k, cc):
         def source():
-            return order[k], y, c
-
-        arrive(source(), h)
-        launch(source, below_me, h, 0, False, lambda: (order[k] > z) & (z > 0))
-        launch(source, above_me, h, 1, False, lambda: (order[k] < z) & (z < LINES - 1))
-        if not (k == 1 and h == 1):
-            launch(source, to_across, h, 2)
-        launch(source, to_beside, h, 3)
-
-    def opposite(k, h):
+            return order[k], y, cc
+
+        for part in range(PARTS):
+            arrive(source(), c, part)
+            launch(source, below_me, my_side, part, 0, False, lambda: (order[k] > z) & (z > 0))
+            launch(source, above_me, my_side, part, 1, False, lambda: (order[k] < z) & (z < LINES - 1))
+            if not (k == 1 and cc == 1):
+                launch(source, to_across, my_side, part, 2)
+            launch(source, to_beside, my_side, part, 3)
+
+    def opposite(k, cc):
         def source():
-            return order[k], 1 - y, c
-
-        arrive(source(), h)
-        if k == 0 and h == 1:
-            launch(source, lambda: (order[1], y, c), h, 4)
-        launch(source, to_beside, h, 3)
-
-    def twin(k, dy, h):
-        arrive((order[k], lax.rem(y + dy, 2), 1 - c), h)
-
-    def stage(ref, sem, low, first, last):
-        return pltpu.make_async_copy(
-            land.at[pl.ds(first * rows, (last - first) * rows)],
-            ref.at[pl.ds((first - low) * rows, (last - first) * rows)],
-            stage_sems.at[sem],
-        )
-
-    for h in range(HALVES):
-        column(1, h)
-        opposite(0, h)
-    for h in range(HALVES):
-        twin(0, 0, h)
-        twin(0, 1, h)
-    stage(early, 0, 0, 1, 4).start()
-    for h in range(HALVES):
-        column(2, h)
-        opposite(1, h)
-    for h in range(HALVES):
-        twin(1, 0, h)
-    stage(early, 1, 0, 4, 6).start()
-    for h in range(HALVES):
-        twin(1, 1, h)
-        twin(2, 0, h)
-    stage(early, 2, 0, 6, FIRST).start()
+            return order[k], 1 - y, cc
+
+        for part in range(PARTS):
+            arrive(source(), c, part)
+            launch(source, to_beside, my_side, part, 3)
+
+    def level():
+        for part in range(PARTS):
+            launch(lambda: (z, 1 - y, 1), lambda: (order[1], y, c), my_side, part, 4)
+
+    def twin(k, dy, cc):
+        for part in range(PARTS):
+            arrive((order[k], lax.rem(y + dy, 2), cc), 1 - c, part)
+
+    def kinds(inner, outer):
+        kept = len(started)
+
+        @pl.when(middle)
+        def _():
+            for event, args in inner:
+                event(*args)
+
+        del started[kept:]
+
+        @pl.when(edge)
+        def _():
+            for event, args in outer:
+                event(*args)
+
+    def stage(sem, first, last):
+        place = pl.ds(first * rows, (last - first) * rows)
+        return pltpu.make_async_copy(land.at[place], ready.at[place], stage_sems.at[sem])
+
+    for part in range(PARTS):
+        arrive((z, y, 1 - c), 1 - c, part)
+    beside_place = pl.ds(pl.multiple_of((1 - c) * rows, rows), rows)
+    beside_copy = pltpu.make_async_copy(land.at[beside_place], ready.at[beside_place], stage_sems.at[0])
+    beside_copy.start()
+    columns = [(column, (1, 0)), (column, (1, 1)), (column, (2, 0)), (column, (2, 1))]
+    columns += [(column, (3, 0)), (column, (3, 1))]
+    across = [(opposite, (0, 0)), (opposite, (0, 1)), (opposite, (1, 0)), (opposite, (2, 0))]
+    rebalance = (level, ())
+    inner = [columns[0], columns[2], across[0], columns[1], columns[3], across[1]]
+    inner += [columns[4], across[2], columns[5], rebalance, across[3]]
+    outer = [columns[0], across[0], columns[1], across[1], rebalance]
+    outer += [columns[2], across[2], columns[3], across[3]]
+    kinds(inner, outer)
+    for k, dy, cc in ((0, 1, 0), (0, 1, 1), (1, 0, 0), (1, 0, 1), (1, 1, 0)):
+        twin(k, dy, cc)
+    stage(1, 2, 7).start()
+    for k, dy, cc in ((2, 0, 0), (2, 0, 1), (2, 1, 0)):
+        twin(k, dy, cc)
+    stage(2, 8, 11).start()
 
     def gathered(k, carry):
         peer = lax.rem(me + k, count)
@@ -485,72 +552,58 @@
         return carry
 
     lax.fori_loop(1, count, gathered, 0)
-    sums = jnp.sum(parts[...], axis=0)
+    sums = jnp.sum(tallies[...], axis=0)
     total = rows * BLOCK * count
     mean = sums[0:1, :] / total
     stats[0:1, :] = mean
     stats[1:2, :] = lax.rsqrt(sums[1:2, :] / total - mean * mean + 1e-05)
 
-    for copy in own_copies:
+    own_copies[1].wait()
+    beside_copy.wait()
+    stage(1, 2, 7).wait()
+    stage(2, 8, 11).wait()
+    for copy in loads[2:]:
         copy.wait()
-    stage(early, 0, 0, 1, 4).wait()
-    stage(early, 1, 0, 4, 6).wait()
-    stage(early, 2, 0, 6, FIRST).wait()
 
     chunk_rows = STEP * BLOCK
     chunks = tiles * NSEL // STEP
-    share_of = chunks // 8
+    share_of = chunks // 4
+
+    def advance(sem, first, last):
+        copy = stage(sem, first, last)
+        copy.start()
+        copy.wait()
 
     def chunk(i, carry):
-        @pl.when(i == share_of - 1)
-        def _():
-            column(3, 0)
-
         @pl.when(i == share_of)
         def _():
-            opposite(2, 0)
-
-        @pl.when(i == 2 * share_of - 1)
-        def _():
-            column(3, 1)
+            opposite(2, 1)
+            kinds([], [columns[4]])
+            twin(2, 1, 1)
+            twin(3, 0, 0)
+            advance(3, 11, 13)
 
         @pl.when(i == 2 * share_of)
         def _():
-            opposite(2, 1)
-            for h in range(HALVES):
-                twin(2, 1, h)
-                twin(3, 0, h)
-            stage(later, 3, FIRST, FIRST, SECOND).start()
-            stage(later, 3, FIRST, FIRST, SECOND).wait()
-
-        @pl.when(i == 4 * share_of)
-        def _():
+            kinds([], [columns[5]])
             opposite(3, 0)
-
-        @pl.when(i == 5 * share_of)
+            twin(3, 1, 0)
+            twin(3, 0, 1)
+            advance(4, 13, 15)
+
+        @pl.when(i == 3 * share_of)
         def _():
             opposite(3, 1)
-
-        @pl.when(i == 6 * share_of)
-        def _():
-            for h in range(HALVES):
-                twin(3, 1, h)
-
-        @pl.when(i < 2 * share_of)
+            opposite(1, 1)
+            twin(3, 1, 1)
+            twin(1, 1, 1)
+
+        @pl.when(i < 3 * share_of)
         def _():
             for u in range(STEP):
-                feed[u] = early[plan_s[2, i * STEP + u]]
-
-        @pl.when((i >= 2 * share_of) & (i < 6 * share_of))
-        def _():
-            for u in range(STEP):
-                n = i * STEP + u
-                spot = jnp.full(feed.shape[1:], plan_s[1, n], jnp.int32)
-                feed[u] = jnp.where(
-                    spot < FIRST * obs_blocks, early[plan_s[2, n]], later[plan_s[3, n]]
-                )
-
-        @pl.when(i >= 6 * share_of)
+                feed[u] = ready[plan_s[1, i * STEP + u]]
+
+        @pl.when(i >= 3 * share_of)
         def _():
             for u in range(STEP):
                 feed[u] = land[plan_s[1, i * STEP + u]]
@@ -657,13 +710,18 @@
     return pl.pallas_call(
         fused_kernel,
         out_shape=jax.ShapeDtypeStruct(shape, bf16),
-        in_specs=[vmem, smem, vmem, smem] + [vmem] * 8,
+        in_specs=[vmem, smem, vmem, smem, vmem] + [pl.BlockSpec(memory_space=pl.ANY)] * 7,
         out_specs=vmem,
         scratch_shapes=[
             pltpu.VMEM((SIDES * rows, BLOCK, feat), bf16),
-            pltpu.VMEM((FIRST * rows, BLOCK, feat), bf16),
-            pltpu.VMEM(((SECOND - FIRST) * rows, BLOCK, feat), bf16),
+            pltpu.VMEM(((SIDES - 1) * rows, BLOCK, feat), bf16),
             pltpu.VMEM((STEP, BLOCK, feat), bf16),
+            pltpu.VMEM((tokens, width), bf16),
+            pltpu.VMEM((feat, width), bf16),
+            pltpu.VMEM((width, width), bf16),
+            pltpu.VMEM((width, width), bf16),
+            pltpu.VMEM((width, width), bf16),
+            pltpu.VMEM((width, width), bf16),
             pltpu.VMEM((entries, BLOCK, width), bf16),
             pltpu.VMEM((entries, BLOCK, width), bf16),
             pltpu.VMEM((tokens, width), bf16),
@@ -674,14 +732,15 @@
             pltpu.VMEM((8, feat), jnp.float32),
             pltpu.VMEM((count, 8, feat), jnp.float32),
             pltpu.VMEM((8, feat), jnp.float32),
-            dma((5, HALVES * count)),
-            dma((HALVES * count,)),
+            dma((5, count * CORES * PARTS)),
+            dma((count * CORES * PARTS,)),
             dma((count,)),
             dma((count,)),
             dma((tiles * count,)),
             dma((tiles * count,)),
             dma((2,)),
-            dma((4,)),
+            dma((5,)),
+            dma((6,)),
             dma,
         ],
         compiler_params=pltpu.CompilerParams(
@@ -692,10 +751,10 @@
         counts,
         position[None],
         proc_order,
+        b_obs[None],
+        obs_features.reshape(rows, BLOCK, feat),
         grid_tokens,
-        obs_features.reshape(rows, BLOCK, feat),
         w_obs,
-        b_obs[None],
         w_query,
         w_key,
         w_value,

time: 91 us -> 84.4 us (0.927)
  Pallas kernels: 89 us -> 82.3 us
    pallas_call x1, Pallas kernels: 89 us -> 82.3 us  [fused(): pl.pallas_call(fused_kernel, out_shape=jax.ShapeDtypeStruct(shape, bf16),...]
where the time goes in v2:
time: 84.4 us; the launch traced here: 84.2 us
  Pallas kernels  82.3 us (98%)
  local copies, waits for them, and re-layouts  1.87 us (2%)
    pallas_call x1, Pallas kernels, fused(): pl.pallas_call(fused_kernel, out_shape=jax.ShapeDtypeStruct(shape, bf16),...  82.3 us
    unnamed x1, local copies, waits for them, and re-layouts  1.87 us

profile of v2, /device:TPU:0, one launch (start us, length us, event | category | flops | bytes accessed | tf_op | source)
XLA Modules:
  0.0 84.2 jit_solution(376571962685391718)
XLA Ops:
  0.0 82.3 %shard_map.118 = bf16[64,8,512]{2,1,0:T(8,128)(2,1)} custom-call(s32[32,64]{1,0:T(8,128)} %bitcast.7, s32[64]{0:T(128)} %count_ref.1, s32[1,512]{1,0:T(1,128)} %bitcast.8, s32[64]{0:T(128)} %order_ref.1, f32[1,512]{1,0:T(1,128)} %bitcast.9, bf16[32,64,128]{2,1,0:T(8,128)(2,1)} %bitcast.6, bf16[512,512]{1,0:T(8,128)(2,1)} %grid_hbm.1, ...), custom_call_target="tpu_custom_call" | custom-call | tf_op jit(solution)/shard_map/pallas_call | solution.py:710
  82.3 1.9 %copy.14 = bf16[512,512]{1,0:T(8,128)(2,1)} copy(bf16[512,512]{1,0:T(8,128)(2,1)} %bitcast.5) | data formatting | bytes 1048576

commit v3 on v2

--- a/solution.py
+++ b/solution.py
@@ -218,7 +218,8 @@
 SIDES = LINES * 4
 CORES = 2
 PARTS = 1
-STEP = 8
+STEP = 32
+SUB = 4
 
 
 def reorder(k, z):
@@ -565,7 +566,6 @@
     for copy in loads[2:]:
         copy.wait()
 
-    chunk_rows = STEP * BLOCK
     chunks = tiles * NSEL // STEP
     share_of = chunks // 4
 
@@ -608,16 +608,25 @@
             for u in range(STEP):
                 feed[u] = land[plan_s[1, i * STEP + u]]
 
-        feats = feed[...].reshape(chunk_rows, feed.shape[2]).astype(jnp.float32)
-        normed = ((feats - stats[0:1, :]) * stats[1:2, :]).astype(jnp.bfloat16)
-        hidden = jnp.dot(normed, w_obs_ref[...], preferred_element_type=jnp.float32)
-        hidden = hidden + b_obs_ref[...]
-        embedded = jax.nn.gelu(hidden, approximate=True).astype(jnp.bfloat16)
-        place = pl.ds(i * STEP, STEP)
-        key_rows = jnp.dot(embedded, w_key_ref[...], preferred_element_type=jnp.float32)
-        keys[place] = key_rows.astype(jnp.bfloat16).reshape(STEP, BLOCK, width)
-        value_rows = jnp.dot(embedded, w_value_ref[...], preferred_element_type=jnp.float32)
-        values[place] = value_rows.astype(jnp.bfloat16).reshape(STEP, BLOCK, width)
+        def embed(n):
+            feats = feed[n * SUB : (n + 1) * SUB].reshape(SUB * BLOCK, feed.shape[2])
+            normed = (feats.astype(jnp.float32) - stats[0:1, :]) * stats[1:2, :]
+            hidden = jnp.dot(
+                normed.astype(jnp.bfloat16), w_obs_ref[...], preferred_element_type=jnp.float32
+            )
+            hidden = hidden + b_obs_ref[...]
+            return jax.nn.gelu(hidden, approximate=True).astype(jnp.bfloat16)
+
+        ahead = embed(0)
+        for n in range(STEP // SUB):
+            embedded = ahead
+            if n + 1 < STEP // SUB:
+                ahead = embed(n + 1)
+            place = pl.ds(i * STEP + n * SUB, SUB)
+            key_rows = jnp.dot(embedded, w_key_ref[...], preferred_element_type=jnp.float32)
+            keys[place] = key_rows.astype(jnp.bfloat16).reshape(SUB, BLOCK, width)
+            value_rows = jnp.dot(embedded, w_value_ref[...], preferred_element_type=jnp.float32)
+            values[place] = value_rows.astype(jnp.bfloat16).reshape(SUB, BLOCK, width)
         return carry
 
     lax.fori_loop(0, chunks, chunk, 0)
@@ -628,12 +637,12 @@
     zero = jnp.zeros((), jnp.bfloat16)
     piece = TILE_ROWS // count
 
-    def out_copy(t, source, peer, k):
+    def out_copy(t, source, peer):
         return pltpu.make_async_remote_copy(
             src_ref=encoded.at[t, peer],
             dst_ref=arrived.at[source * tiles + t],
-            send_sem=out_sends.at[t * count + k],
-            recv_sem=out_recvs.at[source * tiles + t],
+            send_sem=out_sends,
+            recv_sem=out_recvs,
             device_id={"tile": peer},
             device_id_type=MESH,
         )
@@ -644,30 +653,36 @@
         bias = jnp.where(key_index < used, 0.0, NEG).astype(jnp.float32)
         places = [plan_s[0, t * NSEL + j] for j in range(NSEL)]
         outs = []
-        for p in range(HEADS // 2):
+
+        def score(p):
             columns = slice(p * pair, (p + 1) * pair)
             q = queries[pl.ds(pl.multiple_of(t * TILE_ROWS, TILE_ROWS), TILE_ROWS), columns]
             both = jnp.concatenate([jnp.where(first, q, zero), jnp.where(first, zero, q)], axis=0)
             key_rows = jnp.concatenate([keys[place, :, columns] for place in places], axis=0)
-            value_rows = jnp.concatenate([values[place, :, columns] for place in places], axis=0)
             scores = lax.dot_general(
                 both, key_rows, (((1,), (1,)), ((), ())), preferred_element_type=jnp.float32
             )
-            scores = jnp.concatenate([scores[:, :certain], scores[:, certain:] + bias], axis=1)
+            return jnp.concatenate([scores[:, :certain], scores[:, certain:] + bias], axis=1)
+
+        ahead = score(0)
+        for p in range(HEADS // 2):
+            scores = ahead
+            if p + 1 < HEADS // 2:
+                ahead = score(p + 1)
+            columns = slice(p * pair, (p + 1) * pair)
+            value_rows = jnp.concatenate([values[place, :, columns] for place in places], axis=0)
+            value_rows = jnp.concatenate([value_rows, jnp.ones_like(value_rows)], axis=1)
             peak = jnp.max(scores, axis=-1, keepdims=True)
-            expo = jnp.exp(scores - peak)
-            totals = jnp.sum(expo, axis=-1, keepdims=True)
-            mixed = jnp.dot(
-                expo.astype(jnp.bfloat16), value_rows, preferred_element_type=jnp.float32
-            )
-            mixed = mixed / totals
+            expo = jnp.exp(scores - peak).astype(jnp.bfloat16)
+            mixed = jnp.dot(expo, value_rows, preferred_element_type=jnp.float32)
+            mixed = mixed[:, :pair] / mixed[:, pair:]
             outs.append(jnp.where(first, mixed[:TILE_ROWS], mixed[TILE_ROWS:]).astype(jnp.bfloat16))
         attended = jnp.concatenate(outs, axis=1)
         result = jnp.dot(attended, w_out_ref[...], preferred_element_type=jnp.float32)
         encoded[t] = result.astype(jnp.bfloat16).reshape(count, piece, width)
 
         def start(k, carry):
-            out_copy(t, me, lax.rem(me + k, count), k).start()
+            out_copy(t, me, lax.rem(me + k, count)).start()
             return carry
 
         lax.fori_loop(1, count, start, 0)
@@ -679,14 +694,9 @@
     for issue in started:
         issue(True)
 
-    def finish(n, carry):
-        t, k = n // (count - 1), 1 + lax.rem(n, count - 1)
-        peer = lax.rem(me + k, count)
-        out_copy(t, peer, peer, k).wait_send()
-        out_copy(t, peer, peer, k).wait_recv()
-        return carry
-
-    lax.fori_loop(0, tiles * (count - 1), finish, 0)
+    for sem in (out_sends, out_recvs):
+        moved = arrived.at[pl.ds(0, tiles * (count - 1))]
+        pltpu.make_async_copy(moved, moved, sem).wait()
 
     def arrange(j, carry):
         out_ref[pl.ds(j, 1)] = arrived[pl.ds(order_ref[j], 1)]
@@ -736,8 +746,8 @@
             dma((count * CORES * PARTS,)),
             dma((count,)),
             dma((count,)),
-            dma((tiles * count,)),
-            dma((tiles * count,)),
+            dma,
+            dma,
             dma((2,)),
             dma((5,)),
             dma((6,)),

time: 84.4 us -> 78.1 us (0.925)
  Pallas kernels: 82.3 us -> 76.1 us
    pallas_call x1, Pallas kernels: 82.3 us -> 76.1 us  [fused(): pl.pallas_call(fused_kernel, out_shape=jax.ShapeDtypeStruct(shape, bf16),...]
where the time goes in v3:
time: 78.1 us; the launch traced here: 77.9 us
  Pallas kernels  76.1 us (97%)
  local copies, waits for them, and re-layouts  1.87 us (2%)
    pallas_call x1, Pallas kernels, fused(): pl.pallas_call(fused_kernel, out_shape=jax.ShapeDtypeStruct(shape, bf16),...  76.1 us
    unnamed x1, local copies, waits for them, and re-layouts  1.87 us

profile of v3, /device:TPU:0, one launch (start us, length us, event | category | flops | bytes accessed | tf_op | source)
XLA Modules:
  0.0 77.9 jit_solution(9210018137555144961)
XLA Ops:
  0.0 76.1 %shard_map.118 = bf16[64,8,512]{2,1,0:T(8,128)(2,1)} custom-call(s32[32,64]{1,0:T(8,128)} %bitcast.7, s32[64]{0:T(128)} %count_ref.1, s32[1,512]{1,0:T(1,128)} %bitcast.8, s32[64]{0:T(128)} %order_ref.1, f32[1,512]{1,0:T(1,128)} %bitcast.9, bf16[32,64,128]{2,1,0:T(8,128)(2,1)} %bitcast.6, bf16[512,512]{1,0:T(8,128)(2,1)} %grid_hbm.1, ...), custom_call_target="tpu_custom_call" | custom-call | tf_op jit(solution)/shard_map/pallas_call | solution.py:720
  76.1 1.9 %copy.14 = bf16[512,512]{1,0:T(8,128)(2,1)} copy(bf16[512,512]{1,0:T(8,128)(2,1)} %bitcast.5) | data formatting | bytes 1048576

commit v4 on v3

--- a/solution.py
+++ b/solution.py
@@ -275,11 +275,10 @@
 
 
 def fused_kernel(
-    lists_ref,
-    count_ref,
-    position_ref,
-    order_ref,
-    b_obs_ref,
+    lists_hbm,
+    count_hbm,
+    position_hbm,
+    b_obs_hbm,
     obs_ref,
     grid_hbm,
     w_obs_hbm,
@@ -287,10 +286,14 @@
     w_key_hbm,
     w_value_hbm,
     w_out_hbm,
-    out_ref,
+    arrived,
     land,
     ready,
     feed,
+    lists_ref,
+    count_ref,
+    position_ref,
+    b_obs_ref,
     grid_ref,
     w_obs_ref,
     w_query_ref,
@@ -301,7 +304,6 @@
     values,
     queries,
     encoded,
-    arrived,
     plan,
     plan_s,
     tally,
@@ -317,6 +319,7 @@
     stage_sems,
     load_sems,
     plan_sem,
+    kept_sems,
 ):
     count = SIDES
     me = lax.axis_index("tile")
@@ -336,6 +339,10 @@
         pltpu.make_async_copy(source, target, load_sems.at[i])
         for i, (source, target) in enumerate(
             (
+                (lists_hbm, lists_ref),
+                (count_hbm, count_ref),
+                (position_hbm, position_ref),
+                (b_obs_hbm, b_obs_ref),
                 (grid_hbm, grid_ref),
                 (w_query_hbm, w_query_ref),
                 (w_obs_hbm, w_obs_ref),
@@ -468,11 +475,11 @@
 
     lax.fori_loop(1, count, share, 0)
 
+    for copy in loads[:6]:
+        copy.wait()
     plan_entries(me, lists_ref, count_ref, position_ref, plan, tiles, obs_blocks)
     plan_copy = pltpu.make_async_copy(plan, plan_s, plan_sem)
     plan_copy.start()
-    loads[0].wait()
-    loads[1].wait()
     queries[...] = jnp.dot(
         grid_ref[...], w_query_ref[...], preferred_element_type=jnp.float32
     ).astype(jnp.bfloat16) * jnp.bfloat16(1.0 / (width // HEADS) ** 0.5)
@@ -563,7 +570,7 @@
     beside_copy.wait()
     stage(1, 2, 7).wait()
     stage(2, 8, 11).wait()
-    for copy in loads[2:]:
+    for copy in loads[6:]:
         copy.wait()
 
     chunks = tiles * NSEL // STEP
@@ -645,6 +652,11 @@
             recv_sem=out_recvs,
             device_id={"tile": peer},
             device_id_type=MESH,
+        )
+
+    def kept_copy(t):
+        return pltpu.make_async_copy(
+            encoded.at[t, me], arrived.at[me * tiles + t], kept_sems.at[t]
         )
 
     def attend_tile(t, carry):
@@ -686,7 +698,7 @@
             return carry
 
         lax.fori_loop(1, count, start, 0)
-        arrived[pl.ds(me * tiles + t, 1)] = encoded[t, pl.ds(me, 1)]
+        kept_copy(t).start()
         return carry
 
     lax.fori_loop(0, tiles, attend_tile, 0)
@@ -698,11 +710,23 @@
         moved = arrived.at[pl.ds(0, tiles * (count - 1))]
         pltpu.make_async_copy(moved, moved, sem).wait()
 
-    def arrange(j, carry):
-        out_ref[pl.ds(j, 1)] = arrived[pl.ds(order_ref[j], 1)]
-        return carry
-
-    lax.fori_loop(0, count * tiles, arrange, 0, unroll=8)
+    for t in range(tiles):
+        kept_copy(t).wait()
+
+
+def arrange_kernel(order_ref, arrived, out):
+    for j in range(out.shape[0]):
+        out[j] = arrived[order_ref[j]]
+
+
+def arrange(arrived, proc_order):
+    vmem = pl.BlockSpec(memory_space=pltpu.VMEM)
+    return pl.pallas_call(
+        arrange_kernel,
+        out_shape=jax.ShapeDtypeStruct(arrived.shape, arrived.dtype),
+        in_specs=[pl.BlockSpec(memory_space=pltpu.SMEM), vmem],
+        out_specs=vmem,
+    )(proc_order, arrived)
 
 
 def fused(lists, counts, position, proc_order, grid_tokens, obs_features, w_obs, b_obs, w_query, w_key, w_value, w_out):
@@ -713,19 +737,21 @@
     piece = TILE_ROWS // count
     entries = tiles * NSEL
     shape = (count * tiles, piece, width)
-    vmem = pl.BlockSpec(memory_space=pltpu.VMEM)
-    smem = pl.BlockSpec(memory_space=pltpu.SMEM)
     bf16 = jnp.bfloat16
     dma = pltpu.SemaphoreType.DMA
-    return pl.pallas_call(
+    arrived = pl.pallas_call(
         fused_kernel,
         out_shape=jax.ShapeDtypeStruct(shape, bf16),
-        in_specs=[vmem, smem, vmem, smem, vmem] + [pl.BlockSpec(memory_space=pl.ANY)] * 7,
-        out_specs=vmem,
+        in_specs=[pl.BlockSpec(memory_space=pltpu.HBM)] * 11,
+        out_specs=pl.BlockSpec(memory_space=pltpu.HBM),
         scratch_shapes=[
             pltpu.VMEM((SIDES * rows, BLOCK, feat), bf16),
             pltpu.VMEM(((SIDES - 1) * rows, BLOCK, feat), bf16),
             pltpu.VMEM((STEP, BLOCK, feat), bf16),
+            pltpu.VMEM((NSEL, count * tiles), jnp.int32),
+            pltpu.SMEM(counts.shape, jnp.int32),
+            pltpu.VMEM((1, position.shape[0]), jnp.int32),
+            pltpu.VMEM((1, width), jnp.float32),
             pltpu.VMEM((tokens, width), bf16),
             pltpu.VMEM((feat, width), bf16),
             pltpu.VMEM((width, width), bf16),
@@ -736,7 +762,6 @@
             pltpu.VMEM((entries, BLOCK, width), bf16),
             pltpu.VMEM((tokens, width), bf16),
             pltpu.VMEM((tiles, count, piece, width), bf16),
-            pltpu.VMEM(shape, bf16),
             pltpu.VMEM((8, entries), jnp.int32),
             pltpu.SMEM((8, entries), jnp.int32),
             pltpu.VMEM((8, feat), jnp.float32),
@@ -750,8 +775,9 @@
             dma,
             dma((2,)),
             dma((5,)),
-            dma((6,)),
+            dma((10,)),
             dma,
+            dma((tiles,)),
         ],
         compiler_params=pltpu.CompilerParams(
             collective_id=0, has_side_effects=True, vmem_limit_bytes=62 * 2**20
@@ -760,7 +786,6 @@
         lists.T,
         counts,
         position[None],
-        proc_order,
         b_obs[None],
         obs_features.reshape(rows, BLOCK, feat),
         grid_tokens,
@@ -769,7 +794,8 @@
         w_key,
         w_value,
         w_out,
-    ).reshape(count * tiles * piece, width)
+    )
+    return arrange(arrived, proc_order).reshape(count * tiles * piece, width)
 
 
 def exchange(obs_features, block_lists, block_counts, block_position, tile_count, own_index):

time: 78.1 us -> 77.4 us (level)
  local copies, waits for them, and re-layouts: 1.87 us -> 0 us
  Pallas kernels: 76.1 us -> 77.3 us
    pallas_call x0 -> x1, Pallas kernels: none -> 1.9 us  [arrange(): pl.pallas_call(arrange_kernel, out_shape=jax.ShapeDtypeStruct(arrived.sha...]
    unnamed x1 -> x0, local copies, waits for them, and re-layouts: 1.87 us -> none
where the time goes in v4:
time: 77.4 us; the launch traced here: 77.3 us
  Pallas kernels  77.3 us (100%)
    pallas_call x1, Pallas kernels, fused(): pl.pallas_call(fused_kernel, out_shape=jax.ShapeDtypeStruct(shape, bf16),...  75.4 us
    pallas_call x1, Pallas kernels, arrange(): pl.pallas_call(arrange_kernel, out_shape=jax.ShapeDtypeStruct(arrived.sha...  1.9 us

profile of v4, /device:TPU:0, one launch (start us, length us, event | category | flops | bytes accessed | tf_op | source)
XLA Modules:
  0.0 77.3 jit_solution(15690280697900834927)
XLA Ops:
  0.0 75.4 %shard_map.118.arrived = bf16[64,8,512]{2,1,0:T(8,128)(2,1)} custom-call(s32[32,64]{1,0:T(8,128)} %bitcast.6, s32[64]{0:T(128)} %count_hbm.1, s32[1,512]{1,0:T(1,128)} %bitcast.7, f32[1,512]{1,0:T(1,128)} %bitcast.8, bf16[32,64,128]{2,1,0:T(8,128)(2,1)} %bitcast.5, bf16[512,512]{1,0:T(8,128)(2,1)} %grid_hbm.1, bf16[128,512]{1,0:T(8,128)(2,1)} %w_obs_hbm.1, ...), custom_call_target="tpu_custom_call" | custom-call | tf_op jit(solution)/shard_map/pallas_call | solution.py:742
  75.4 1.9 %shard_map.119 = bf16[64,8,512]{2,1,0:T(8,128)(2,1)} custom-call(s32[64]{0:T(128)} %order_ref.1, bf16[64,8,512]{2,1,0:T(8,128)(2,1)} %shard_map.118.arrived), custom_call_target="tpu_custom_call" | custom-call | tf_op jit(solution)/shard_map/pallas_call | solution.py:724

commit v5 on v4

--- a/solution.py
+++ b/solution.py
@@ -697,7 +697,7 @@
             out_copy(t, me, lax.rem(me + k, count)).start()
             return carry
 
-        lax.fori_loop(1, count, start, 0)
+        lax.fori_loop(1, count, start, 0, unroll=5)
         kept_copy(t).start()
         return carry
 

time: 77.4 us -> 77.1 us (level)
  no operation moved by 1% of the time
where the time goes in v5:
time: 77.1 us; the launch traced here: 77 us
  Pallas kernels  77 us (100%)
    pallas_call x1, Pallas kernels, fused(): pl.pallas_call(fused_kernel, out_shape=jax.ShapeDtypeStruct(shape, bf16),...  75.1 us
    pallas_call x1, Pallas kernels, arrange(): pl.pallas_call(arrange_kernel, out_shape=jax.ShapeDtypeStruct(arrived.sha...  1.9 us

profile of v5, /device:TPU:0, one launch (start us, length us, event | category | flops | bytes accessed | tf_op | source)
XLA Modules:
  0.0 77.0 jit_solution(12950346006444192392)
XLA Ops:
  0.0 75.1 %shard_map.118.arrived = bf16[64,8,512]{2,1,0:T(8,128)(2,1)} custom-call(s32[32,64]{1,0:T(8,128)} %bitcast.6, s32[64]{0:T(128)} %count_hbm.1, s32[1,512]{1,0:T(1,128)} %bitcast.7, f32[1,512]{1,0:T(1,128)} %bitcast.8, bf16[32,64,128]{2,1,0:T(8,128)(2,1)} %bitcast.5, bf16[512,512]{1,0:T(8,128)(2,1)} %grid_hbm.1, bf16[128,512]{1,0:T(8,128)(2,1)} %w_obs_hbm.1, ...), custom_call_target="tpu_custom_call" | custom-call | tf_op jit(solution)/shard_map/pallas_call | solution.py:742
  75.1 1.9 %shard_map.119 = bf16[64,8,512]{2,1,0:T(8,128)(2,1)} custom-call(s32[64]{0:T(128)} %order_ref.1, bf16[64,8,512]{2,1,0:T(8,128)(2,1)} %shard_map.118.arrived), custom_call_target="tpu_custom_call" | custom-call | tf_op jit(solution)/shard_map/pallas_call | solution.py:724
